TPU v7x, 32 devices: a whole 2x2x4 slice. The times are simulated.
32 devices in a mesh: leaf: 4 (over x, core), blk: 8 (over z, y).
Axes of the slice: x: 2, y: 2, z: 4, core: 2. Of those that a mesh axis runs over, the one named last changes fastest.
Arguments:
- right_side: float32 [4, 8, 448, 128], P('leaf', 'blk'), may hold values from -6 to 6
- inverse_blocks: bfloat16 [4, 8, 448, 2048], P('leaf', 'blk'), may hold values from -0.125 to 0.125
- coupling: bfloat16 [4, 8, 640, 1024], P('leaf', 'blk'), may hold values from -0.0625 to 0.0625
- update_rows: int32 [10, 1024], replicated, may hold values from 0 to 2047, as said below
Outputs:
- solution: float32 [4, 8, 448, 128], P('leaf', 'blk')
Inputs may be any that keep to these rules, and one draw needn't show every extreme that they name: `update_rows`: the 1024 entries of each row are distinct.
All inputs are finite; a program needn't handle non-finite values.
Results may differ from a plain program's by a relative error of at most 0.0075.
Values may be sent and summed in bfloat16 or wider, within the bound.
No kernel may reach another device: no remote copies, remote signals or barrier semaphores. Data moves between devices by JAX's collectives and lax.ppermute only.
A program may use at most 64 MiB of HBM per device.

v0:
```python
import jax
import jax.numpy as jnp
from jax import lax
from jax.sharding import PartitionSpec as P


def from_partner(shard, axis, distance):
    return lax.ppermute(shard, axis, [(i, i ^ 1 << distance) for i in range(lax.axis_size(axis))])


def group_total(partial_value, level_no, leaf_id, want_full):
    members = partial_value.shape[0]
    member = leaf_id & members - 1
    full_rows = None
    summed = lax.psum_scatter(partial_value, "blk", scatter_dimension=1, tiled=True)
    for bit_no in range(level_no):
        summed = summed + from_partner(summed, "leaf", bit_no)
    own_rows = lax.dynamic_index_in_dim(summed, member, 0, keepdims=False)[0]
    if want_full:
        full_rows = lax.all_gather(summed.astype(jnp.bfloat16), "blk", axis=1, tiled=True)
    if full_rows is not None:
        full_rows = full_rows.reshape(-1, full_rows.shape[-1])
    return (own_rows, full_rows)


def local(right_side, inverse_blocks, coupling, update_rows):
    leaves = lax.axis_size("leaf")
    blocks = lax.axis_size("blk")
    tree_depth = leaves.bit_length() - 1
    leaf_id = lax.axis_index("leaf")
    blk_id = lax.axis_index("blk")
    node_width = inverse_blocks.shape[-1]
    load_cases = right_side.shape[-1]
    local_rhs = right_side[0, 0]
    local_inverse = inverse_blocks[0, 0]
    local_coupling = coupling[0, 0]
    row_counts = [node_width // (blocks << level_no) for level_no in range(tree_depth + 1)]
    row_starts = [sum(row_counts[:level_no]) for level_no in range(tree_depth + 1)]
    coupling_starts = {}
    cursor = 0
    for level_no in range(tree_depth):
        for ancestor in range(level_no + 1, tree_depth + 1):
            coupling_starts[level_no, ancestor] = cursor
            cursor += row_counts[level_no]
    pair_bases = []
    cursor = 0
    for level_no in range(tree_depth + 1):
        pair_bases.append(cursor)
        cursor += (leaves >> level_no) * (tree_depth - level_no)

    def coupling_block(level_no, ancestor):
        coup_start = coupling_starts[level_no, ancestor]
        return local_coupling[coup_start : coup_start + row_counts[level_no]]

    def row_list(level_no, ancestor):
        node_id = leaf_id >> level_no
        pair_row = (
            pair_bases[level_no] + node_id * (tree_depth - level_no) + (ancestor - level_no - 1)
        )
        return lax.dynamic_index_in_dim(update_rows, pair_row, 0, keepdims=False)

    pending = {}
    y_levels = []
    for level_no in range(tree_depth + 1):
        members = 1 << level_no
        row_count = row_counts[level_no]
        row_start = row_starts[level_no]
        member = leaf_id & members - 1
        if level_no == 0:
            residual = lax.all_gather(
                local_rhs[row_start : row_start + row_count].astype(jnp.bfloat16),
                "blk",
                axis=0,
                tiled=True,
            )
        else:
            buffer = pending.get(level_no, jnp.zeros((node_width, load_cases), jnp.float32))
            slot_start = (member * blocks + blk_id) * row_count
            current = lax.dynamic_slice_in_dim(buffer, slot_start, row_count, 0)
            buffer = lax.dynamic_update_slice_in_dim(
                buffer, current + local_rhs[row_start : row_start + row_count], slot_start, 0
            )
            unused_rows, residual = group_total(
                buffer.reshape(members, blocks, row_count, load_cases), level_no, leaf_id, True
            )
        inverse_rows = local_inverse[row_start : row_start + row_count]
        y_rows = jnp.dot(inverse_rows, residual, preferred_element_type=jnp.float32)
        y_levels.append(y_rows)
        y_round = y_rows.astype(jnp.bfloat16)
        for ancestor in range(level_no + 1, tree_depth + 1):
            contrib = lax.dot_general(
                coupling_block(level_no, ancestor),
                y_round,
                (((0,), (0,)), ((), ())),
                preferred_element_type=jnp.float32,
            )
            summed = pending.get(ancestor, jnp.zeros((node_width, load_cases), jnp.float32))
            pending[ancestor] = summed.at[row_list(level_no, ancestor)].add(-contrib)
    solved = {}
    outputs = [None] * (tree_depth + 1)
    for level_no in range(tree_depth, -1, -1):
        members = 1 << level_no
        row_count = row_counts[level_no]
        row_start = row_starts[level_no]
        z_rows = y_levels[level_no]
        for ancestor in range(level_no + 1, tree_depth + 1):
            picked = jnp.take(solved[ancestor], row_list(level_no, ancestor), axis=0)
            z_rows = z_rows - jnp.dot(
                coupling_block(level_no, ancestor), picked, preferred_element_type=jnp.float32
            )
        inverse_rows = local_inverse[row_start : row_start + row_count]
        partial_value = lax.dot_general(
            inverse_rows,
            z_rows.astype(jnp.bfloat16),
            (((0,), (0,)), ((), ())),
            preferred_element_type=jnp.float32,
        )
        own_rows, full_rows = group_total(
            partial_value.reshape(members, blocks, row_count, load_cases),
            level_no,
            leaf_id,
            level_no > 0,
        )
        outputs[level_no] = own_rows
        if level_no > 0:
            solved[level_no] = full_rows
    return jnp.concatenate(outputs, 0)[None, None]


def solution(mesh):
    in_specs = (
        P("leaf", "blk", None, None),
        P("leaf", "blk", None, None),
        P("leaf", "blk", None, None),
        P(),
    )
    out_specs = P("leaf", "blk", None, None)
    return jax.shard_map(local, mesh=mesh, in_specs=in_specs, out_specs=out_specs, check_vma=False)
```

profile of v0, /device:TPU:0, one launch (start us, length us, event | category | flops | bytes accessed | tf_op | source)
XLA Modules:
  0.0 612.2 jit_solution(16145240339841454955)
XLA Ops:
  7.6 33.0 %all-gather = bf16[1,1,2048,128]{3,2,1,0:T(8,128)(2,1)S(1)} all-gather(bf16[1,1,256,128]{3,2,1,0:T(8,128)(2,1)S(1)} %slice.135), channel_id=2, replica_groups=mesh['leaf'=4,'blk'=8] {'blk'}, dimensions={2}, use_global_device_ids=true | all-gather | bytes 589824 | tf_op jit(solution)/shard_map/all_gather | solution.py:70
  40.6 1.6 fusion.8
  44.2 6.3 %scatter_custom_fusion = f32[2048,128]{1,0:T(8,128)S(1)} fusion(s32[1024]{0:T(1024)S(1)} %bitcast.138, f32[1024,128]{1,0:T(8,128)S(1)} %copy.20, f32[]{:T(128)} %constant.56.clone.1), kind=kCustom, calls=%fused_computation.38 | custom fusion | flops 131072 | bytes 1048580 | tf_op jit(solution)/shard_map/scatter-add | solution.py:98
  53.1 78.9 %all-reduce.7.cloned.1.call-done = f32[2,8,128,128]{3,2,1,0:T(8,128)} async-done(((f32[2,8,128,128]{3,2,1,0:T(8,128)}), f32[2,8,128,128]{3,2,1,0:T(8,128)}) %all-reduce.7.cloned.1.call-update) | async-done | bytes 1048592
  132.0 2.2 constant_dynamic-slice_fusion.5
  134.7 6.5 %scatter_custom_fusion.1 = f32[2048,128]{1,0:T(8,128)S(1)} fusion(s32[1024]{0:T(1024)} %bitcast.137, f32[1024,128]{1,0:T(8,128)S(1)} %copy.21, f32[]{:T(128)} %constant.56.clone.1), kind=kCustom, calls=%fused_computation.36 | custom fusion | flops 131072 | bytes 1049088 | tf_op jit(solution)/shard_map/scatter-add | solution.py:98
  141.3 1.6 add_convert_fusion.1
  142.9 31.4 %all_gather.16 = bf16[2,8,128,128]{3,2,1,0:T(8,128)(2,1)S(1)} all-gather(bf16[2,1,128,128]{3,2,1,0:T(8,128)(2,1)S(1)} %add_convert_fusion.1), channel_id=1, replica_groups=mesh['leaf'=4,'blk'=8] {'blk'}, dimensions={1}, use_global_device_ids=true | all-gather | bytes 589824 | tf_op jit(solution)/shard_map/all_gather | solution.py:20
  174.6 2.0 fusion
  177.8 6.4 %scatter_fusion = f32[2048,128]{1,0:T(8,128)S(1)} fusion(f32[2048,128]{1,0:T(8,128)S(1)} %scatter_custom_fusion.1, s32[1024]{0:T(1024)S(1)} %bitcast.136, f32[1024,128]{1,0:T(8,128)S(1)} %copy.22), kind=kCustom, calls=%fused_computation.5 | custom fusion | flops 131072 | bytes 1576960 | tf_op jit(solution)/shard_map/scatter-add | solution.py:98
  186.1 77.9 %all-reduce.9.cloned.1.call-done = f32[4,8,64,128]{3,2,1,0:T(8,128)} async-done(((f32[4,8,64,128]{3,2,1,0:T(8,128)}), f32[4,8,64,128]{3,2,1,0:T(8,128)}) %all-reduce.9.cloned.1.call-update) | async-done | bytes 1048592
  264.0 1.6 constant_dynamic-slice_fusion.4
  267.0 1.6 fusion.75
  268.6 1.5 collective-permute-start.2
  270.1 4.1 collective-permute-done.2
  274.2 31.3 %all_gather.17 = bf16[4,8,64,128]{3,2,1,0:T(8,128)(2,1)S(1)} all-gather(bf16[4,1,64,128]{3,2,1,0:T(8,128)(2,1)S(1)} %add_convert_fusion), channel_id=1, replica_groups=mesh['leaf'=4,'blk'=8] {'blk'}, dimensions={1}, use_global_device_ids=true | all-gather | bytes 589824 | tf_op jit(solution)/shard_map/all_gather | solution.py:20
  307.5 78.2 %all-reduce.11.cloned.1.call-done = f32[4,8,64,128]{3,2,1,0:T(8,128)} async-done(((f32[4,8,64,128]{3,2,1,0:T(8,128)}), f32[4,8,64,128]{3,2,1,0:T(8,128)}) %all-reduce.11.cloned.1.call-update) | async-done | bytes 1048592
  385.6 1.6 constant_dynamic-slice_fusion.3
  388.6 1.6 fusion.74
  390.2 1.5 collective-permute-start.4
  391.8 4.1 collective-permute-done.4
  395.9 31.3 %all_gather.18 = bf16[4,8,64,128]{3,2,1,0:T(8,128)(2,1)S(1)} all-gather(bf16[4,1,64,128]{3,2,1,0:T(8,128)(2,1)S(1)} %get-tuple-element.8), channel_id=1, replica_groups=mesh['leaf'=4,'blk'=8] {'blk'}, dimensions={1}, use_global_device_ids=true | all-gather | bytes 589824 | tf_op jit(solution)/shard_map/all_gather | solution.py:20
  427.1 3.2 gather_fusion
  430.4 2.0 convolution_bitcast_fusion.2
  434.0 64.1 %reduce-scatter.12.cloned.1.call-done = f32[2,1,128,128]{3,2,0,1:T(8,128)} async-done(((f32[2,8,128,128]{3,2,0,1:T(8,128)}), f32[2,1,128,128]{3,2,0,1:T(8,128)}) %reduce-scatter.12.cloned.1.call-update) | async-done | bytes 131088 | tf_op jit(solution)/shard_map/reduce_scatter | solution.py:15
  498.1 3.2 gather_fusion.2
  501.4 31.5 %all_gather.19 = bf16[2,8,128,128]{3,2,0,1:T(8,128)(2,1)S(1)} all-gather(bf16[2,1,128,128]{3,2,0,1:T(8,128)(2,1)S(1)} %get-tuple-element.6), channel_id=1, replica_groups=mesh['leaf'=4,'blk'=8] {'blk'}, dimensions={1}, use_global_device_ids=true | all-gather | bytes 589824 | tf_op jit(solution)/shard_map/all_gather | solution.py:20
  532.9 3.2 gather_fusion.1
  536.1 1.5 fusion.4
  537.6 1.8 convolution_bitcast_fusion
  540.8 63.3 %reduce-scatter.14.cloned.1.call-done = f32[1,1,256,128]{3,2,1,0:T(8,128)} async-done(((f32[1,8,256,128]{3,2,1,0:T(8,128)}), f32[1,1,256,128]{3,2,1,0:T(8,128)}) %reduce-scatter.14.cloned.1.call-update) | async-done | bytes 131088 | tf_op jit(solution)/shard_map/reduce_scatter | solution.py:15
  604.1 1.6 maximum_bitcast_fusion
  (63 shorter events, 17.3 us)
Async XLA Ops:
  6.5 125.5 %all-reduce.7.cloned.1.call-start = ((), (), s32[]{:S(2)}) async-start(), calls=%async_computation.4 | async-start | bytes 2097152
  6.5 35.7 %copy-start.4 = (bf16[1,1,640,1024]{3,2,1,0:T(8,128)(2,1)S(1)}, bf16[1,1,640,1024]{3,2,1,0:T(8,128)(2,1)}, u32[]{:S(2)}) copy-start(bf16[1,1,640,1024]{3,2,1,0:T(8,128)(2,1)} %param.8) | copy-start | bytes 3932164
  42.2 92.0 %copy-start.5 = (f32[256,128]{1,0:T(8,128)}, f32[256,128]{1,0:T(8,128)S(1)}, u32[]{:S(2)}) copy-start(f32[256,128]{1,0:T(8,128)S(1)} %fusion.8) | copy-start | bytes 393220
  42.7 9.7 %copy-start.8 = (u32[32]{0:T(128)S(1)}, u32[32]{0:T(128)}, u32[]{:S(2)}) copy-start(u32[32]{0:T(128)} %constant.76) | copy-start | bytes 388
  51.3 1.0 copy-start.1
  52.3 211.6 %all-reduce.9.cloned.1.call-start = ((), (), s32[]{:S(2)}) async-start(), calls=%async_computation.5 | async-start | bytes 2097152
  134.2 7.0 %collective-permute-start = (f32[2,1,128,128]{3,2,1,0:T(8,128)}, f32[2,1,128,128]{3,2,1,0:T(8,128)S(1)}, u32[]{:S(2)}, u32[]{:S(2)}) collective-permute-start(f32[2,1,128,128]{3,2,1,0:T(8,128)} %constant_dynamic-slice_fusion.5), channel_id=1, source_target_pairs={{0,8},{8,0},{16,24},{24,16},{1,9},{9,1},{17,25},{25,17},{2,10},{10... | collective-permute-start | bytes 393224 | tf_op jit(solution)/shard_map/ppermute | solution.py:8
  134.5 39.8 %copy-start.2 = (bf16[1,1,448,2048]{3,2,1,0:T(8,128)(2,1)S(1)}, bf16[1,1,448,2048]{3,2,1,0:T(8,128)(2,1)}, u32[]{:S(2)}) copy-start(bf16[1,1,448,2048]{3,2,1,0:T(8,128)(2,1)} %param.7) | copy-start | bytes 5505028
  185.0 1.0 copy-start
  186.1 199.6 %all-reduce.11.cloned.1.call-start = ((), (), s32[]{:S(2)}) async-start(), calls=%async_computation.6 | async-start | bytes 2097152
  265.6 1.4 collective-permute-start.1
  268.6 5.6 collective-permute-start.2
  307.4 190.7 %reduce-scatter.12.cloned.1.call-start = ((), (), s32[]{:S(2)}) async-start(), calls=%async_computation.2 | async-start | bytes 1179648 | tf_op jit(solution)/shard_map/reduce_scatter | solution.py:15
  387.2 1.4 collective-permute-start.3
  390.2 5.6 collective-permute-start.4
  434.0 170.1 %reduce-scatter.14.cloned.1.call-start = ((), (), s32[]{:S(2)}) async-start(), calls=%async_computation.3 | async-start | bytes 1179648 | tf_op jit(solution)/shard_map/reduce_scatter | solution.py:15
  498.1 3.2 copy-start.7
  498.1 3.2 collective-permute-start.5
  532.9 3.2 copy-start.6
  532.9 4.7 copy-start.3
Sparse Core Ops, SparseCore 0:
  52.5 79.4 all-reduce.6
  186.2 77.7 all-reduce.8
  307.5 78.0 all-reduce.10
  434.1 63.9 reduce-scatter.11
  540.9 63.1 reduce-scatter.13
where the time goes:
time: 613 us; the launch traced here: 612 us
  waiting for transfers between devices  373 us (61%)
  blocking collectives  158 us (26%)
  other arithmetic  28.8 us (5%)
  local copies, waits for them, and re-layouts  24.7 us (4%)
  between operations  13.5 us (2%)
  matrix products  10.2 us (2%)
    unnamed x8, waiting for transfers between devices  235 us
    reduce_scatter x2, waiting for transfers between devices, group_total(): lax.psum_scatter(partial_value, 'blk', scatter_dimension=1, tiled=True)  127 us
    all_gather x4, blocking collectives, group_total(): lax.all_gather(summed.astype(jnp.bfloat16), 'blk', axis=1, tiled=True)  125 us
    all_gather x1, blocking collectives, local(): lax.all_gather(local_rhs[row_start:row_start + row_count].astype(jnp.bflo...  33 us
    scatter-add x3, other arithmetic, local(): pending[ancestor] = summed.at[row_list(level_no, ancestor)].add(-contrib)  19.2 us
  transfers between devices with their start and end apart: 11, of which 9 were waited for; matrix products, arithmetic and copies ran while one was open for 2% of the time, Pallas kernels for 0%

commit v1 on v0

--- a/solution.py
+++ b/solution.py
@@ -17,7 +17,12 @@
         summed = summed + from_partner(summed, "leaf", bit_no)
     own_rows = lax.dynamic_index_in_dim(summed, member, 0, keepdims=False)[0]
     if want_full:
-        full_rows = lax.all_gather(summed.astype(jnp.bfloat16), "blk", axis=1, tiled=True)
+        full_rows = jnp.concatenate(
+            lax.all_to_all(
+                jnp.stack([summed.astype(jnp.bfloat16)] * lax.axis_size("blk")), "blk", 0, 0
+            ),
+            axis=1,
+        )
     if full_rows is not None:
         full_rows = full_rows.reshape(-1, full_rows.shape[-1])
     return (own_rows, full_rows)

time: 613 us -> 554 us (0.904)
  blocking collectives: 158 us -> 51 us
  waiting for transfers between devices: 373 us -> 406 us
  starting transfers between devices: 3.38 us -> 15.5 us
    all_gather x4 -> x0, blocking collectives: 125 us -> none  [group_total(): lax.all_gather(summed.astype(jnp.bfloat16), 'blk', axis=1, tiled=True)]
    all_to_all x0 -> x3, waiting for transfers between devices: none -> 32.2 us  [group_total(): lax.all_to_all(jnp.stack([summed.astype(jnp.bfloat16)] * lax.axis_size('b...]
    all_to_all x0 -> x1, blocking collectives: none -> 17.9 us  [group_total(): lax.all_to_all(jnp.stack([summed.astype(jnp.bfloat16)] * lax.axis_size('b...]
    all_to_all x0 -> x3, starting transfers between devices: none -> 12 us  [group_total(): lax.all_to_all(jnp.stack([summed.astype(jnp.bfloat16)] * lax.axis_size('b...]
  transfers between devices with their start and end apart: 11 -> 14, of which waited for: 9 -> 14; matrix products, arithmetic and copies ran while one was open for 2% -> 2% of each run, Pallas kernels for 0% -> 0%
where the time goes in v1:
time: 554 us; the launch traced here: 553 us
  waiting for transfers between devices  406 us (73%)
  blocking collectives  51 us (9%)
  other arithmetic  29.2 us (5%)
  local copies, waits for them, and re-layouts  27.5 us (5%)
  starting transfers between devices  15.5 us (3%)
  between operations  13.5 us (2%)
  matrix products  10.2 us (2%)
    unnamed x8, waiting for transfers between devices  234 us
    reduce_scatter x2, waiting for transfers between devices, group_total(): lax.psum_scatter(partial_value, 'blk', scatter_dimension=1, tiled=True)  127 us
    all_gather x1, blocking collectives, local(): lax.all_gather(local_rhs[row_start:row_start + row_count].astype(jnp.bflo...  33 us
    all_to_all x3, waiting for transfers between devices, group_total(): lax.all_to_all(jnp.stack([summed.astype(jnp.bfloat16)] * lax.axis_size('b...  32.2 us
    scatter-add x3, other arithmetic, local(): pending[ancestor] = summed.at[row_list(level_no, ancestor)].add(-contrib)  19.5 us
    all_to_all x1, blocking collectives, group_total(): lax.all_to_all(jnp.stack([summed.astype(jnp.bfloat16)] * lax.axis_size('b...  17.9 us
    ppermute x6, waiting for transfers between devices, from_partner(): lax.ppermute(shard, axis, [(i, i ^ 1 << distance) for i in range(lax.axis...  13.7 us
    all_to_all x3, starting transfers between devices, group_total(): lax.all_to_all(jnp.stack([summed.astype(jnp.bfloat16)] * lax.axis_size('b...  12 us
  transfers between devices with their start and end apart: 14, of which 14 were waited for; matrix products, arithmetic and copies ran while one was open for 2% of the time, Pallas kernels for 0%

profile of v1, /device:TPU:0, one launch (start us, length us, event | category | flops | bytes accessed | tf_op | source)
XLA Modules:
  0.0 553.4 jit_solution(11021629262132525457)
XLA Ops:
  7.6 33.0 %all-gather = bf16[1,1,2048,128]{3,2,1,0:T(8,128)(2,1)S(1)} all-gather(bf16[1,1,256,128]{3,2,1,0:T(8,128)(2,1)S(1)} %slice.135), channel_id=2, replica_groups=mesh['leaf'=4,'blk'=8] {'blk'}, dimensions={2}, use_global_device_ids=true | all-gather | bytes 589824 | tf_op jit(solution)/shard_map/all_gather | solution.py:75
  40.6 1.6 fusion.8
  43.6 6.3 %scatter_custom_fusion = f32[2048,128]{1,0:T(8,128)S(1)} fusion(s32[1024]{0:T(1024)S(1)} %bitcast.159, f32[1024,128]{1,0:T(8,128)S(1)} %copy.19, f32[]{:T(128)} %constant.56.clone.1), kind=kCustom, calls=%fused_computation.38 | custom fusion | flops 131072 | bytes 1048580 | tf_op jit(solution)/shard_map/scatter-add | solution.py:103
  52.4 79.0 %all-reduce.7.cloned.1.call-done = f32[2,8,128,128]{3,2,1,0:T(8,128)} async-done(((f32[2,8,128,128]{3,2,1,0:T(8,128)}), f32[2,8,128,128]{3,2,1,0:T(8,128)}) %all-reduce.7.cloned.1.call-update) | async-done | bytes 1048592
  131.4 1.5 constant_dynamic-slice_fusion.4
  134.4 1.5 fusion.57
  136.8 4.2 all-to-all-start
  142.3 6.8 %scatter_custom_fusion.1 = f32[2048,128]{1,0:T(8,128)S(1)} fusion(s32[1024]{0:T(1024)S(1)} %bitcast.158, f32[1024,128]{1,0:T(8,128)} %copy.21, f32[]{:T(128)} %constant.56.clone.1), kind=kCustom, calls=%fused_computation.36 | custom fusion | flops 131072 | bytes 1049088 | tf_op jit(solution)/shard_map/scatter-add | solution.py:103
  149.1 6.7 %all-to-all-done = bf16[8,2,1,128,128]{4,3,1,2,0:T(8,128)(2,1)S(1)} async-done(((bf16[8,2,1,128,128]{4,3,1,2,0:T(8,128)(2,1)}), bf16[8,2,1,128,128]{4,3,1,2,0:T(8,128)(2,1)S(1)}, u32[]{:S(2)}, u32[]{:S(2)}) %all-to-all-start) | async-done | bytes 524320 | tf_op jit(solution)/shard_map/all_to_all | solution.py:21
  156.2 2.0 fusion
  159.4 6.4 %scatter_fusion = f32[2048,128]{1,0:T(8,128)S(1)} fusion(f32[2048,128]{1,0:T(8,128)S(1)} %scatter_custom_fusion.1, s32[1024]{0:T(1024)S(1)} %bitcast.157, f32[1024,128]{1,0:T(8,128)S(1)} %copy.22), kind=kCustom, calls=%fused_computation.5 | custom fusion | flops 131072 | bytes 1576960 | tf_op jit(solution)/shard_map/scatter-add | solution.py:103
  167.7 77.4 %all-reduce.9.cloned.1.call-done = f32[4,8,64,128]{3,2,1,0:T(8,128)} async-done(((f32[4,8,64,128]{3,2,1,0:T(8,128)}), f32[4,8,64,128]{3,2,1,0:T(8,128)}) %all-reduce.9.cloned.1.call-update) | async-done | bytes 1048592
  245.1 1.5 constant_dynamic-slice_fusion.3
  248.0 1.5 fusion.75
  251.1 4.1 collective-permute-done.2
  255.3 17.9 %all_to_all.20 = bf16[8,4,1,64,128]{4,3,1,2,0:T(8,128)(2,1)S(1)} all-to-all(bf16[8,4,1,64,128]{4,3,1,2,0:T(8,128)(2,1)S(1)} %stack.9), channel_id=1, replica_groups=mesh['leaf'=4,'blk'=8] {'blk'}, dimensions={0} | all-to-all | bytes 1048576 | tf_op jit(solution)/shard_map/all_to_all | solution.py:21
  275.2 77.5 %all-reduce.11.cloned.1.call-done = f32[4,8,64,128]{3,2,1,0:T(8,128)} async-done(((f32[4,8,64,128]{3,2,1,0:T(8,128)}), f32[4,8,64,128]{3,2,1,0:T(8,128)}) %all-reduce.11.cloned.1.call-update) | async-done | bytes 1048592
  355.6 1.6 fusion.74
  358.7 4.1 collective-permute-done.4
  363.7 4.2 all-to-all-start.2
  368.0 13.9 %all-to-all-done.2 = bf16[8,4,1,64,128]{4,3,1,2,0:T(8,128)(2,1)S(1)} async-done(((bf16[8,4,1,64,128]{4,3,1,2,0:T(8,128)(2,1)}), bf16[8,4,1,64,128]{4,3,1,2,0:T(8,128)(2,1)S(1)}, u32[]{:S(2)}, u32[]{:S(2)}) %all-to-all-start.2) | async-done | bytes 524320 | tf_op jit(solution)/shard_map/all_to_all | solution.py:21
  382.0 3.2 gather_fusion
  385.2 2.0 convolution_bitcast_fusion.2
  388.8 63.4 %reduce-scatter.12.cloned.1.call-done = f32[2,1,128,128]{3,2,0,1:T(8,128)} async-done(((f32[2,8,128,128]{3,2,0,1:T(8,128)}), f32[2,1,128,128]{3,2,0,1:T(8,128)}) %reduce-scatter.12.cloned.1.call-update) | async-done | bytes 131088 | tf_op jit(solution)/shard_map/reduce_scatter | solution.py:15
  452.2 1.6 collective-permute-done.5
  455.5 3.6 all-to-all-start.3
  459.3 3.2 gather_fusion.2
  462.5 11.6 %all-to-all-done.3 = bf16[8,2,1,128,128]{4,3,1,2,0:T(8,128)(2,1)S(1)} async-done(((bf16[8,2,1,128,128]{4,3,1,2,0:T(8,128)(2,1)}), bf16[8,2,1,128,128]{4,3,1,2,0:T(8,128)(2,1)S(1)}, u32[]{:S(2)}, u32[]{:S(2)}) %all-to-all-start.3) | async-done | bytes 524320 | tf_op jit(solution)/shard_map/all_to_all | solution.py:21
  474.1 3.2 gather_fusion.1
  478.8 1.8 convolution_bitcast_fusion
  482.0 63.2 %reduce-scatter.14.cloned.1.call-done = f32[1,1,256,128]{3,2,1,0:T(8,128)} async-done(((f32[1,8,256,128]{3,2,1,0:T(8,128)}), f32[1,1,256,128]{3,2,1,0:T(8,128)}) %reduce-scatter.14.cloned.1.call-update) | async-done | bytes 131088 | tf_op jit(solution)/shard_map/reduce_scatter | solution.py:15
  545.2 1.6 maximum_bitcast_fusion
  (70 shorter events, 28.6 us)
Async XLA Ops:
  6.5 124.9 %all-reduce.7.cloned.1.call-start = ((), (), s32[]{:S(2)}) async-start(), calls=%async_computation.8 | async-start | bytes 2097152
  6.5 35.7 %copy-start.4 = (bf16[1,1,640,1024]{3,2,1,0:T(8,128)(2,1)S(1)}, bf16[1,1,640,1024]{3,2,1,0:T(8,128)(2,1)}, u32[]{:S(2)}) copy-start(bf16[1,1,640,1024]{3,2,1,0:T(8,128)(2,1)} %param.8) | copy-start | bytes 3932164
  42.2 98.8 %copy-start.5 = (f32[256,128]{1,0:T(8,128)}, f32[256,128]{1,0:T(8,128)S(1)}, u32[]{:S(2)}) copy-start(f32[256,128]{1,0:T(8,128)S(1)} %fusion.8) | copy-start | bytes 393220
  42.7 9.1 %copy-start.7 = (u32[32]{0:T(128)S(1)}, u32[32]{0:T(128)}, u32[]{:S(2)}) copy-start(u32[32]{0:T(128)} %constant.76) | copy-start | bytes 388
  50.7 1.0 copy-start.1
  132.9 1.4 collective-permute-start
  136.8 19.0 %all-to-all-start = ((bf16[8,2,1,128,128]{4,3,1,2,0:T(8,128)(2,1)}), bf16[8,2,1,128,128]{4,3,1,2,0:T(8,128)(2,1)S(1)}, u32[]{:S(2)}, u32[]{:S(2)}) async-start(bf16[8,2,1,128,128]{4,3,1,2,0:T(8,128)(2,1)} %stack.8), calls=%async_computation | async-start | bytes 1048576 | tf_op jit(solution)/shard_map/all_to_all | solution.py:21
  141.0 104.1 %all-reduce.9.cloned.1.call-start = ((), (), s32[]{:S(2)}) async-start(), calls=%async_computation.9 | async-start | bytes 2097152
  142.3 13.5 %copy-start.2 = (bf16[1,1,448,2048]{3,2,1,0:T(8,128)(2,1)S(1)}, bf16[1,1,448,2048]{3,2,1,0:T(8,128)(2,1)}, u32[]{:S(2)}) copy-start(bf16[1,1,448,2048]{3,2,1,0:T(8,128)(2,1)} %param.7) | copy-start | bytes 5505028
  166.6 1.0 copy-start
  167.6 185.0 %all-reduce.11.cloned.1.call-start = ((), (), s32[]{:S(2)}) async-start(), calls=%async_computation.10 | async-start | bytes 2097152
  246.6 1.4 collective-permute-start.1
  249.6 5.6 %collective-permute-start.2 = (f32[4,1,64,128]{3,2,1,0:T(8,128)S(1)}, f32[4,1,64,128]{3,2,1,0:T(8,128)S(1)}, u32[]{:S(2)}, u32[]{:S(2)}) collective-permute-start(f32[4,1,64,128]{3,2,1,0:T(8,128)S(1)} %fusion.75), channel_id=1, source_target_pairs={{0,16},{8,24},{16,0},{24,8},{1,17},{9,25},{17,1},{25,9},{2,18},{10... | collective-permute-start | bytes 393224 | tf_op jit(solution)/shard_map/ppermute | solution.py:8
  354.2 1.4 collective-permute-start.3
  357.2 5.6 %collective-permute-start.4 = (f32[4,1,64,128]{3,2,0,1:T(8,128)S(1)}, f32[4,1,64,128]{3,2,0,1:T(8,128)S(1)}, u32[]{:S(2)}, u32[]{:S(2)}) collective-permute-start(f32[4,1,64,128]{3,2,0,1:T(8,128)S(1)} %fusion.74), channel_id=1, source_target_pairs={{0,16},{8,24},{16,0},{24,8},{1,17},{9,25},{17,1},{25,9},{2,18},{10... | collective-permute-start | bytes 393224 | tf_op jit(solution)/shard_map/ppermute | solution.py:8
  363.7 18.2 %all-to-all-start.2 = ((bf16[8,4,1,64,128]{4,3,1,2,0:T(8,128)(2,1)}), bf16[8,4,1,64,128]{4,3,1,2,0:T(8,128)(2,1)S(1)}, u32[]{:S(2)}, u32[]{:S(2)}) async-start(bf16[8,4,1,64,128]{4,3,1,2,0:T(8,128)(2,1)} %stack.10), calls=%async_computation.2 | async-start | bytes 1048576 | tf_op jit(solution)/shard_map/all_to_all | solution.py:21
  367.9 84.2 %reduce-scatter.12.cloned.1.call-start = ((), (), s32[]{:S(2)}) async-start(), calls=%async_computation.6 | async-start | bytes 1179648 | tf_op jit(solution)/shard_map/reduce_scatter | solution.py:15
  452.2 1.6 collective-permute-start.5
  455.5 18.5 %all-to-all-start.3 = ((bf16[8,2,1,128,128]{4,3,1,2,0:T(8,128)(2,1)}), bf16[8,2,1,128,128]{4,3,1,2,0:T(8,128)(2,1)S(1)}, u32[]{:S(2)}, u32[]{:S(2)}) async-start(bf16[8,2,1,128,128]{4,3,1,2,0:T(8,128)(2,1)} %stack.11), calls=%async_computation.4 | async-start | bytes 1048576 | tf_op jit(solution)/shard_map/all_to_all | solution.py:21
  459.2 86.0 %reduce-scatter.14.cloned.1.call-start = ((), (), s32[]{:S(2)}) async-start(), calls=%async_computation.7 | async-start | bytes 1179648 | tf_op jit(solution)/shard_map/reduce_scatter | solution.py:15
  474.1 3.2 copy-start.6
  474.1 4.7 copy-start.3
Sparse Core Ops, SparseCore 0:
  51.9 79.4 all-reduce.6
  167.8 77.2 all-reduce.8
  275.3 77.2 all-reduce.10
  388.9 63.2 reduce-scatter.11
  482.1 63.1 reduce-scatter.13
